TPU v7x, 256 devices: a whole 4x4x8 slice. The times are simulated.
256 devices in a mesh: subcube: 2 (over y_hi), row: 8 (over z), col: 16 (over x, y_lo, core).
Axes of the slice: x: 4, y: 4 (y_hi: 2, y_lo: 2; y = y_hi * 2 + y_lo), z: 8, core: 2. Of those that a mesh axis runs over, the one named last changes fastest.
Arguments:
- front_entries: float32 [16, 8, 64, 24576], P('col', 'row', None, 'subcube'), may hold values from -6 to 6
- child_blocks: float32 [2, 16, 8, 64, 12288], P('subcube', 'col', 'row'), may hold values from -6 to 6
- row_maps: int32 [2, 12288], replicated, may hold values from 0 to 24575, as said below
- pivot_inverses: float32 [2, 512, 512], P(None, 'row')
- tile_mask: int32 [48, 16], P(('subcube', 'row'), 'col'), may hold values 0 or 1
Outputs:
- factored: float32 [24576, 8192], P(('subcube', 'row'), 'col')
Inputs may be any that keep to these rules, and one draw needn't show every extreme that they name: Each row of row_maps lists 12288 distinct front rows in increasing order; its first is 0 and its last 24575.
All inputs are finite; a program needn't handle non-finite values. No bound on the sum of `tile_mask` on one device may be relied on, other than what follows from the above.
Results may differ from a plain program's by a relative error of at most 0.0001.
Values sent between devices are 32-bit elements; how exact they have to be, the bound alone decides.
No kernel may reach another device: no remote copies, remote signals or barrier semaphores. Data moves between devices by JAX's collectives and lax.ppermute only.
A program may use at most 128 MiB of HBM per device.

v0:
```python
import jax
import jax.numpy as jnp
from jax import lax
from jax.sharding import PartitionSpec as P

PANEL = 512
PANELS = 2


def broadcast(value, axis, source):
    kept = jnp.where(lax.axis_index(axis) == source, value, 0).astype(value.dtype)
    return lax.psum(kept, axis)


def from_partner(x, axis, distance):
    return lax.ppermute(x, axis, [(i, i ^ 1 << distance) for i in range(lax.axis_size(axis))])


def product(left, right):
    return jnp.dot(left, right, precision=lax.Precision.HIGHEST, preferred_element_type=jnp.float32)


def extend_add(target, child_rows, row_map, offset):
    local_rows = row_map - offset
    inside = (local_rows >= 0) & (local_rows < target.shape[1])
    target_rows = jnp.where(inside, local_rows, target.shape[1])
    return target.at[:, target_rows].add(child_rows, mode="drop")


def send_strip(row_strip, root_row):
    return broadcast(row_strip, ("subcube", "row"), root_row)


def local(front_entries, child_blocks, row_maps, pivot_inverses, tile_mask):
    half_rows = front_entries.shape[3]
    subcube_side = lax.axis_index("subcube")
    own_block = child_blocks[0, 0, 0]
    partner_block = from_partner(own_block, "subcube", 0)
    own_map = lax.dynamic_index_in_dim(row_maps, subcube_side, 0, keepdims=False)
    partner_map = lax.dynamic_index_in_dim(row_maps, 1 - subcube_side, 0, keepdims=False)
    assembled = front_entries[0, 0]
    assembled = extend_add(assembled, own_block, own_map, subcube_side * half_rows)
    assembled = extend_add(assembled, partner_block, partner_map, subcube_side * half_rows)
    regrouped = lax.all_to_all(assembled, "row", split_axis=1, concat_axis=0, tiled=True)
    local_block = regrouped.T
    row_count = local_block.shape[0]
    block_width = local_block.shape[1]
    column_place = lax.axis_index("col")
    column_ids = column_place * block_width + jnp.arange(block_width, dtype=jnp.int32)
    grid_row = subcube_side * lax.axis_size("row") + lax.axis_index("row")
    row_ids = grid_row * row_count + jnp.arange(row_count, dtype=jnp.int32)
    kept_tiles = jnp.repeat(jnp.repeat(tile_mask.astype(jnp.float32), PANEL, axis=0), PANEL, axis=1)
    for panel_index in range(PANELS):
        first_col = panel_index * PANEL
        after_col = first_col + PANEL
        owner_col = first_col // block_width
        local_start = first_col - owner_col * block_width
        root_row = first_col // row_count
        row_start = first_col - root_row * row_count
        panel_cols = local_block
        row_strip = local_block[row_start : row_start + PANEL, :]
        inverse = lax.all_gather(pivot_inverses[panel_index], "row", axis=0, tiled=True)
        scaled = broadcast(product(panel_cols, inverse), "col", owner_col)
        across = send_strip(row_strip, root_row)
        update = product(scaled, across)
        below = (row_ids >= after_col).astype(jnp.float32)[:, None]
        live_mask = kept_tiles * (column_ids >= after_col).astype(jnp.float32)[None, :] * below
        local_block = local_block - update * live_mask
        current = local_block
        replace = (column_place == owner_col) & (row_ids >= first_col)[:, None]
        local_block = local_block.at[:, local_start : local_start + PANEL].set(
            jnp.where(replace, scaled, current)
        )
    return local_block


def solution(mesh):
    return jax.shard_map(
        local,
        mesh=mesh,
        in_specs=(
            P("col", "row", None, "subcube"),
            P("subcube", "col", "row", None, None),
            P(),
            P(None, "row", None),
            P(("subcube", "row"), "col"),
        ),
        out_specs=P(("subcube", "row"), "col"),
        check_vma=False,
    )
```

profile of v0, /device:TPU:1, one launch (start us, length us, event | category | flops | bytes accessed | tf_op | source)
XLA Modules:
  0.0 864.5 jit_solution(14957715034153878558)
XLA Ops:
  7.4 3.7 collective-permute-start
  11.1 0.0 copy-start
  11.1 5.9 copy.10
  17.0 0.0 copy-done
  17.0 0.0 copy-start.2
  17.0 4.0 copy.11
  21.0 0.0 copy-done.2
  21.0 0.3 compare_select_fusion
  21.3 64.7 %scatter_fusion = f32[64,12288]{0,1:T(8,128)} fusion(f32[64,12288]{0,1:T(8,128)} %bitcast.31, s32[12288]{0:T(1024)S(1)} %bitcast.39, f32[12288,64]{1,0:T(8,128)} %copy.11), kind=kCustom, calls=%fused_computation | custom fusion | flops 786432 | bytes 9486336 | tf_op jit(solution)/shard_map/scatter-add | solution.py:27
  86.1 0.0 collective-permute-done
  86.1 5.8 copy.12
  91.8 64.7 %scatter_fusion.1 = f32[64,12288]{0,1:T(8,128)} fusion(f32[64,12288]{0,1:T(8,128)} %scatter_fusion, s32[12288]{0:T(1024)S(1)} %bitcast.38, f32[12288,64]{1,0:T(8,128)} %copy.12), kind=kCustom, calls=%fused_computation.1 | custom fusion | flops 786432 | bytes 9486336 | tf_op jit(solution)/shard_map/scatter-add | solution.py:27
  156.6 6.1 copy.13
  162.7 0.0 copy-start.1
  162.7 8.3 all-to-all-start
  171.0 0.0 all-gather.5.cloned.1.call-start
  171.0 0.0 copy-done.1
  171.0 0.7 fusion.17
  171.8 0.0 all-gather.5.cloned.1.call-update
  171.8 0.0 all-reduce.7.cloned.1.call-start
  171.8 81.7 %all-to-all-done = f32[64,8,1536]{2,0,1:T(8,128)S(1)} async-done(((f32[64,8,1536]{2,0,1:T(8,128)}), f32[64,8,1536]{2,0,1:T(8,128)S(1)}, u32[]{:S(2)}, u32[]{:S(2)}) %all-to-all-start) | async-done | bytes 3145760 | tf_op jit(solution)/shard_map/all_to_all | solution.py:44
  253.6 2.3 copy.14
  255.9 2.4 slice_select_fusion.1
  258.3 0.0 all-reduce.7.cloned.1.call-update
  258.3 0.2 all-reduce.5.cloned.1.call-start
  258.6 0.0 all-gather.5.cloned.1.call-done
  258.6 12.4 %convolution_select_fusion.1 = f32[1536,512]{1,0:T(8,128)} fusion(f32[512,1536]{1,0:T(8,128)S(1)} %bitcast.34, pred[]{:T(512)S(6)} %eq.13, f32[1,512,512]{2,1,0:T(8,128)} %all-gather.5.cloned.1.call-done), kind=kOutput, calls=%fused_computation.3 | convolution fusion | flops 4832624640 | bytes 7340033 | tf_op jit(solution)/shard_map/dot_general | solution.py:20
  271.0 0.0 copy-start.3
  271.0 0.0 all-reduce.5.cloned.1.call-update
  271.0 0.0 all-gather.7.cloned.1.call-start
  271.0 0.7 all-gather.7.cloned.1.call-update
  271.8 0.0 all-reduce.11.cloned.1.call-start
  271.8 0.0 copy-done.3
  271.8 0.1 broadcast_in_dim.44
  271.9 130.9 %all-reduce.7.cloned.1.call-done = f32[512,512]{1,0:T(8,128)} async-done(((f32[512,512]{1,0:T(8,128)}), f32[512,512]{1,0:T(8,128)}) %all-reduce.7.cloned.1.call-update) | async-done | bytes 1048592 | tf_op jit(solution)/shard_map/psum | solution.py:12
  402.8 142.3 %all-reduce.5.cloned.1.call-done = f32[1536,512]{1,0:T(8,128)} async-done(((f32[1536,512]{1,0:T(8,128)}), f32[1536,512]{1,0:T(8,128)}) %all-reduce.5.cloned.1.call-update) | async-done | bytes 3145744 | tf_op jit(solution)/shard_map/psum | solution.py:12
  545.1 9.6 %fusion.1 = f32[1536,512]{1,0:T(8,128)S(1)} fusion(f32[1536,512]{1,0:T(8,128)} %all-reduce.5.cloned.1.call-done, f32[512,512]{1,0:T(8,128)} %all-reduce.7.cloned.1.call-done, f32[1536]{0:T(1024)S(1)} %get-tuple-element.49, f32[512]{0:T(512)S(1)} %fusion.15, f32[1536]{0:T(1024)S(1)} %broadcast_in_dim.45, pred[1536]{0:T(1024)(128)(4,1)S(1)} %get-tuple-element.50, ...), kind=kOutput, calls=%fused_computation.7 | convolution fusion | flops 4835770368 | bytes 10501632 | tf_op jit(solution)/shard_map/dot_general | solution.py:20
  554.7 1.1 slice_select_fusion
  555.8 0.0 all-reduce.11.cloned.1.call-update
  555.8 0.3 all-reduce.9.cloned.1.call-start
  556.1 0.0 all-gather.7.cloned.1.call-done
  556.1 7.5 convolution_select_fusion
  563.6 0.0 all-reduce.9.cloned.1.call-update
  563.6 141.0 %all-reduce.11.cloned.1.call-done = f32[512,512]{1,0:T(8,128)} async-done(((f32[512,512]{1,0:T(8,128)}), f32[512,512]{1,0:T(8,128)}) %all-reduce.11.cloned.1.call-update) | async-done | bytes 1048592 | tf_op jit(solution)/shard_map/psum | solution.py:12
  704.6 142.5 %all-reduce.9.cloned.1.call-done = f32[1536,512]{1,0:T(8,128)} async-done(((f32[1536,512]{1,0:T(8,128)}), f32[1536,512]{1,0:T(8,128)}) %all-reduce.9.cloned.1.call-update) | async-done | bytes 3145744 | tf_op jit(solution)/shard_map/psum | solution.py:12
  847.1 9.9 %fusion.3 = f32[1536,512]{1,0:T(8,128)} fusion(f32[1536,512]{1,0:T(8,128)} %all-reduce.9.cloned.1.call-done, f32[1536,512]{1,0:T(8,128)S(1)} %fusion.1, f32[512,512]{1,0:T(8,128)} %all-reduce.11.cloned.1.call-done, f32[1536]{0:T(1024)S(1)} %get-tuple-element.52, f32[512]{0:T(512)S(1)} %fusion.16, f32[1536]{0:T(1024)S(1)} %broadcast_in_dim.45, ...), kind=kOutput, calls=%fused_computation.9 | convolution fusion | flops 4835770368 | bytes 10501632 | tf_op jit(solution)/shard_map/dot_general | solution.py:20
  (6 shorter events, 0.0 us)
Async XLA Ops:
  7.4 78.7 %collective-permute-start = (f32[64,12288]{1,0:T(8,128)}, f32[64,12288]{1,0:T(8,128)}, u32[]{:S(2)}, u32[]{:S(2)}) collective-permute-start(f32[64,12288]{1,0:T(8,128)} %bitcast.36), channel_id=1, source_target_pairs={{0,128},{128,0},{1,129},{129,1},{2,130},{130,2},{3,131},{131,3},{4... | collective-permute-start | bytes 9437192 | tf_op jit(solution)/shard_map/ppermute | solution.py:16
  11.1 5.9 copy-start
  17.0 4.0 copy-start.2
  162.7 8.4 copy-start.1
  162.7 90.9 %all-to-all-start = ((f32[64,8,1536]{2,0,1:T(8,128)}), f32[64,8,1536]{2,0,1:T(8,128)S(1)}, u32[]{:S(2)}, u32[]{:S(2)}) async-start(f32[64,8,1536]{2,0,1:T(8,128)} %copy.13), calls=%async_computation | async-start | bytes 6291456 | tf_op jit(solution)/shard_map/all_to_all | solution.py:44
  171.0 87.6 %all-gather.5.cloned.1.call-start = ((), (), s32[]{:S(2)}) async-start(), calls=%async_computation.5 | async-start | bytes 1179648 | tf_op jit(solution)/shard_map/all_gather | solution.py:62
  171.8 231.0 %all-reduce.7.cloned.1.call-start = ((), (), s32[]{:S(2)}) async-start(), calls=%async_computation.2 | async-start | bytes 2097152 | tf_op jit(solution)/shard_map/psum | solution.py:12
  258.3 286.8 %all-reduce.5.cloned.1.call-start = ((), (), s32[]{:S(2)}) async-start(), calls=%async_computation.1 | async-start | bytes 6291456 | tf_op jit(solution)/shard_map/psum | solution.py:12
  271.0 0.8 copy-start.3
  271.0 285.1 %all-gather.7.cloned.1.call-start = ((), (), s32[]{:S(2)}) async-start(), calls=%async_computation.6 | async-start | bytes 1179648 | tf_op jit(solution)/shard_map/all_gather | solution.py:62
  271.8 432.8 %all-reduce.11.cloned.1.call-start = ((), (), s32[]{:S(2)}) async-start(), calls=%async_computation.4 | async-start | bytes 2097152 | tf_op jit(solution)/shard_map/psum | solution.py:12
  555.8 291.3 %all-reduce.9.cloned.1.call-start = ((), (), s32[]{:S(2)}) async-start(), calls=%async_computation.3 | async-start | bytes 6291456 | tf_op jit(solution)/shard_map/psum | solution.py:12
Sparse Core Ops, SparseCore 0:
  173.7 55.4 all-gather.4
  273.6 30.5 all-gather.6
Sparse Core Ops, SparseCore 1:
  258.4 144.4 all-reduce.6
  405.6 139.5 all-reduce.4
  555.9 148.6 all-reduce.10
  707.3 139.7 all-reduce.8
where the time goes:
time: 865 us
  waiting for transfers between devices  639 us (74%)
  other arithmetic  133 us (15%)
  matrix products  39.3 us (5%)
  local copies, waits for them, and re-layouts  24.9 us (3%)
  between operations  15.2 us (2%)
  starting transfers between devices  12.7 us (1%)
    psum x4, waiting for transfers between devices, broadcast(): return lax.psum(kept, axis)  557 us
    scatter-add x2, other arithmetic, extend_add(): return target.at[:, target_rows].add(child_rows, mode='drop')  129 us
    all_to_all x1, waiting for transfers between devices, local(): lax.all_to_all(assembled, 'row', split_axis=1, concat_axis=0, tiled=True)  81.7 us
    dot_general x4, matrix products, product(): jnp.dot(left, right, precision=lax.Precision.HIGHEST, preferred_element_t...  39.3 us
  transfers between devices with their start and end apart: 8, of which 5 were waited for; matrix products, arithmetic and copies ran while one was open for 13% of the time, Pallas kernels for 0%

commit v1 on v0

--- a/solution.py
+++ b/solution.py
@@ -9,7 +9,7 @@
 
 def broadcast(value, axis, source):
     kept = jnp.where(lax.axis_index(axis) == source, value, 0).astype(value.dtype)
-    return lax.psum(kept, axis)
+    return jnp.sum(lax.all_gather(kept, axis), axis=0)
 
 
 def from_partner(x, axis, distance):

time: 865 us -> 1280 us (1.48)
  waiting for transfers between devices: 639 us -> 1000 us
  other arithmetic: 133 us -> 191 us
    all_gather x0 -> x4, waiting for transfers between devices: none -> 915 us  [broadcast(): return jnp.sum(lax.all_gather(kept, axis), axis=0)]
    psum x4 -> x0, waiting for transfers between devices: 557 us -> none  [broadcast(): return lax.psum(kept, axis)]
    reduce_sum x0 -> x4, other arithmetic: none -> 58.2 us  [broadcast(): return jnp.sum(lax.all_gather(kept, axis), axis=0)]
  transfers between devices with their start and end apart: 8 -> 8, of which waited for: 5 -> 6; matrix products, arithmetic and copies ran while one was open for 13% -> 12% of each run, Pallas kernels for 0% -> 0%
where the time goes in v1:
time: 1280 us
  waiting for transfers between devices  1000 us (78%)
  other arithmetic  191 us (15%)
  matrix products  39.1 us (3%)
  local copies, waits for them, and re-layouts  25 us (2%)
  between operations  13.6 us (1%)
    all_gather x4, waiting for transfers between devices, broadcast(): return jnp.sum(lax.all_gather(kept, axis), axis=0)  915 us
    scatter-add x2, other arithmetic, extend_add(): return target.at[:, target_rows].add(child_rows, mode='drop')  129 us
    all_to_all x1, waiting for transfers between devices, local(): lax.all_to_all(assembled, 'row', split_axis=1, concat_axis=0, tiled=True)  81.7 us
    reduce_sum x4, other arithmetic, broadcast(): return jnp.sum(lax.all_gather(kept, axis), axis=0)  58.2 us
    dot_general x4, matrix products, product(): jnp.dot(left, right, precision=lax.Precision.HIGHEST, preferred_element_t...  39.1 us
  transfers between devices with their start and end apart: 8, of which 6 were waited for; matrix products, arithmetic and copies ran while one was open for 12% of the time, Pallas kernels for 0%

profile of v1, /device:TPU:1, one launch (start us, length us, event | category | flops | bytes accessed | tf_op | source)
XLA Modules:
  0.0 1283.8 jit_solution(13825796733814715265)
XLA Ops:
  6.5 3.7 collective-permute-start
  10.3 0.0 copy-start
  10.3 5.9 copy.10
  16.2 0.0 copy-done
  16.2 0.0 copy-start.2
  16.2 4.0 copy.11
  20.2 0.0 copy-done.2
  20.2 0.3 compare_select_fusion
  20.5 64.7 %scatter_fusion = f32[64,12288]{0,1:T(8,128)} fusion(f32[64,12288]{0,1:T(8,128)} %bitcast.35, s32[12288]{0:T(1024)S(1)} %bitcast.47, f32[12288,64]{1,0:T(8,128)} %copy.11), kind=kCustom, calls=%fused_computation | custom fusion | flops 786432 | bytes 9486336 | tf_op jit(solution)/shard_map/scatter-add | solution.py:27
  85.2 0.0 collective-permute-done
  85.2 5.8 copy.12
  91.0 64.7 %scatter_fusion.1 = f32[64,12288]{0,1:T(8,128)} fusion(f32[64,12288]{0,1:T(8,128)} %scatter_fusion, s32[12288]{0:T(1024)S(1)} %bitcast.46, f32[12288,64]{1,0:T(8,128)} %copy.12), kind=kCustom, calls=%fused_computation.1 | custom fusion | flops 786432 | bytes 9486336 | tf_op jit(solution)/shard_map/scatter-add | solution.py:27
  155.7 6.1 copy.13
  161.8 8.3 all-to-all-start
  170.1 0.0 all-gather.13.cloned.1.call-start
  170.2 0.0 copy-done.1
  170.2 0.7 fusion.17
  170.9 0.0 all-gather.13.cloned.1.call-update
  170.9 0.0 all-gather.17.cloned.1.call-start
  171.0 81.7 %all-to-all-done = f32[64,8,1536]{2,0,1:T(8,128)S(1)} async-done(((f32[64,8,1536]{2,0,1:T(8,128)}), f32[64,8,1536]{2,0,1:T(8,128)S(1)}, u32[]{:S(2)}, u32[]{:S(2)}) %all-to-all-start) | async-done | bytes 3145760 | tf_op jit(solution)/shard_map/all_to_all | solution.py:44
  252.7 2.4 copy.14
  255.1 2.3 slice_select_fusion.1
  257.4 0.0 all-gather.17.cloned.1.call-update
  257.4 0.2 all-gather.15.cloned.1.call-start
  257.7 0.0 all-gather.13.cloned.1.call-done
  257.7 12.4 convolution_select_fusion.1
  270.1 0.0 all-gather.15.cloned.1.call-update
  270.1 0.0 all-gather.19.cloned.1.call-start
  270.2 0.5 all-gather.19.cloned.1.call-update
  270.7 0.0 all-gather.23.cloned.1.call-start
  270.7 0.0 copy-done.3
  270.7 0.1 broadcast_in_dim.44
  270.9 206.9 %all-gather.17.cloned.1.call-done = f32[8192,512]{1,0:T(8,128)} async-done(((f32[512,512]{1,0:T(8,128)}), f32[8192,512]{1,0:T(8,128)}) %all-gather.17.cloned.1.call-update) | async-done | bytes 16777232 | tf_op jit(solution)/shard_map/all_gather | solution.py:12
  477.7 8.9 reduce_sum.37
  486.6 242.8 %all-gather.15.cloned.1.call-done = f32[24576,512]{1,0:T(8,128)} async-done(((f32[1536,512]{1,0:T(8,128)}), f32[24576,512]{1,0:T(8,128)}) %all-gather.15.cloned.1.call-update) | async-done | bytes 50331664 | tf_op jit(solution)/shard_map/all_gather | solution.py:12
  729.4 20.2 %reduce_sum.36 = f32[1536,512]{1,0:T(8,128)} reduce(f32[16,1536,512]{2,1,0:T(8,128)} %bitcast.37, f32[]{:T(128)} %constant.114.clone.1), dimensions={0}, to_apply=%region_2.3 | reduce | flops 11796480 | bytes 53477380 | tf_op jit(solution)/shard_map/reduce_sum | solution.py:12
  749.7 9.6 fusion.1
  759.3 1.1 slice_select_fusion
  760.3 0.0 all-gather.23.cloned.1.call-update
  760.4 0.3 all-gather.21.cloned.1.call-start
  760.6 4.4 all-gather.19.cloned.1.call-done
  765.0 7.4 convolution_select_fusion
  772.4 0.0 all-gather.21.cloned.1.call-update
  772.5 223.0 %all-gather.23.cloned.1.call-done = f32[8192,512]{1,0:T(8,128)} async-done(((f32[512,512]{1,0:T(8,128)}), f32[8192,512]{1,0:T(8,128)}) %all-gather.23.cloned.1.call-update) | async-done | bytes 16777232 | tf_op jit(solution)/shard_map/all_gather | solution.py:12
  995.5 8.9 reduce_sum.39
  1004.4 242.7 %all-gather.21.cloned.1.call-done = f32[24576,512]{1,0:T(8,128)} async-done(((f32[1536,512]{1,0:T(8,128)}), f32[24576,512]{1,0:T(8,128)}) %all-gather.21.cloned.1.call-update) | async-done | bytes 50331664 | tf_op jit(solution)/shard_map/all_gather | solution.py:12
  1247.0 20.2 %reduce_sum.38 = f32[1536,512]{1,0:T(8,128)} reduce(f32[16,1536,512]{2,1,0:T(8,128)} %bitcast.38, f32[]{:T(128)} %constant.114.clone.1), dimensions={0}, to_apply=%region_4.5 | reduce | flops 11796480 | bytes 53477380 | tf_op jit(solution)/shard_map/reduce_sum | solution.py:12
  1267.3 9.7 fusion.3
  (8 shorter events, 0.1 us)
Async XLA Ops:
  6.5 78.7 %collective-permute-start = (f32[64,12288]{1,0:T(8,128)}, f32[64,12288]{1,0:T(8,128)}, u32[]{:S(2)}, u32[]{:S(2)}) collective-permute-start(f32[64,12288]{1,0:T(8,128)} %bitcast.44), channel_id=1, source_target_pairs={{0,128},{128,0},{1,129},{129,1},{2,130},{130,2},{3,131},{131,3},{4... | collective-permute-start | bytes 9437192 | tf_op jit(solution)/shard_map/ppermute | solution.py:16
  10.3 5.9 copy-start
  16.2 4.0 copy-start.2
  161.8 8.4 copy-start.1
  161.8 90.9 %all-to-all-start = ((f32[64,8,1536]{2,0,1:T(8,128)}), f32[64,8,1536]{2,0,1:T(8,128)S(1)}, u32[]{:S(2)}, u32[]{:S(2)}) async-start(f32[64,8,1536]{2,0,1:T(8,128)} %copy.13), calls=%async_computation | async-start | bytes 6291456 | tf_op jit(solution)/shard_map/all_to_all | solution.py:44
  170.1 87.5 %all-gather.13.cloned.1.call-start = ((), (), s32[]{:S(2)}) async-start(), calls=%async_computation.1 | async-start | bytes 1179648 | tf_op jit(solution)/shard_map/all_gather | solution.py:62
  170.9 306.8 %all-gather.17.cloned.1.call-start = ((), (), s32[]{:S(2)}) async-start(), calls=%async_computation.3 | async-start | bytes 17825792 | tf_op jit(solution)/shard_map/all_gather | solution.py:12
  257.4 472.0 %all-gather.15.cloned.1.call-start = ((), (), s32[]{:S(2)}) async-start(), calls=%async_computation.2 | async-start | bytes 53477376 | tf_op jit(solution)/shard_map/all_gather | solution.py:12
  270.1 0.7 copy-start.3
  270.1 494.9 %all-gather.19.cloned.1.call-start = ((), (), s32[]{:S(2)}) async-start(), calls=%async_computation.4 | async-start | bytes 1179648 | tf_op jit(solution)/shard_map/all_gather | solution.py:62
  270.7 724.8 %all-gather.23.cloned.1.call-start = ((), (), s32[]{:S(2)}) async-start(), calls=%async_computation.6 | async-start | bytes 17825792 | tf_op jit(solution)/shard_map/all_gather | solution.py:12
  760.4 486.7 %all-gather.21.cloned.1.call-start = ((), (), s32[]{:S(2)}) async-start(), calls=%async_computation.5 | async-start | bytes 53477376 | tf_op jit(solution)/shard_map/all_gather | solution.py:12
Sparse Core Ops, SparseCore 0:
  172.8 55.7 all-gather.12
  257.5 220.1 all-gather.16
  479.6 249.7 all-gather.14
  731.1 33.9 all-gather.18
  767.4 228.0 all-gather.22
  997.2 249.7 all-gather.20
